TPU v7x, 32 devices: a whole 2x2x4 slice. The times are simulated.
32 devices in a mesh: groups: 2 (over y), tgt: 4 (over z), src: 2 (over x), sub: 2 (over core).
Axes of the slice: x: 2, y: 2, z: 4, core: 2. Of those that a mesh axis runs over, the one named last changes fastest.
Arguments:
- points: float32 [3, 4096], P(None, ('groups', 'tgt', 'src', 'sub')), parts along dimension 1, may hold values from -1.4 to 1.4, as said below
- density: float32 [32, 4096], P(None, ('groups', 'tgt', 'src', 'sub')), parts along dimension 1, may hold values from 0.2 to 2
- incident: float32 [32, 4096], P(None, ('groups', 'tgt', 'src', 'sub')), parts along dimension 1, may hold values from -0.21 to 0.21
- precond: float32 [4096], P(('groups', 'tgt', 'src', 'sub')), parts along dimension 0, may hold values from 0.054414064 to 0.16324219
- receivers: int32 [4096], P('groups'), parts along dimension 0, may hold values from 0 to 65535
Outputs:
- density_out: float32 [32, 4096], P(None, ('groups', 'tgt', 'src', 'sub')), parts along dimension 1
- far_field: float32 [32, 4096], P(None, ('groups', 'tgt', 'src', 'sub')), parts along dimension 1
There are 2 independent parts, one for each index of `groups`. A program takes and returns all parts, laid end to end along the dimension named above; each array names one. Nothing has to cross between parts.
Inputs may be any that keep to these rules, and one draw needn't show every extreme that they name: Coordinates of points of a closed star-shaped surface around the anchor. `receivers`: numbers of directions in the receiver table.
All inputs are finite; a program needn't handle non-finite values.
Results may differ from a plain program's by a relative error of at most 0.0015.
Values may be sent and summed in bfloat16 or wider, within the bound.
A program may use at most 64 MiB of HBM per device.

v0:
```python
import functools
import math

import jax
import jax.numpy as jnp
import numpy as np
from jax import lax
from jax.experimental import pallas as pl
from jax.experimental.pallas import tpu as pltpu
from jax.sharding import PartitionSpec as P

ITERS = 4
NDIR = 65536
WAVENUMBER = 32.0
SMOOTHING = 0.02
FOUR_PI = 4.0 * math.pi
TURNS = WAVENUMBER / (2.0 * math.pi)
MAGIC = 12582912.0
LANES = 128
CHUNK = 16
MESH = pl.DeviceIdType.MESH
AXES = ("groups", "tgt", "src", "sub")


def cosine_coefficients(degree):
    fit = np.polynomial.chebyshev.Chebyshev.interpolate(
        lambda u: np.cos(2.0 * np.pi * np.sqrt(u)), degree, domain=[0.0, 0.25]
    )
    return [float(c) for c in fit.convert(kind=np.polynomial.Polynomial).coef]


COSINE = cosine_coefficients(6)


def cos_turns(turns, scale=1.0):
    whole = (turns + MAGIC) - MAGIC
    f = turns - whole
    u = f * f
    total = u * (scale * COSINE[-1]) + scale * COSINE[-2]
    for coefficient in COSINE[-3::-1]:
        total = total * u + scale * coefficient
    return total


def directions(number):
    rotation = ((number >> 8) * 14080 + (number & 255) * 40503) & 65535
    part = rotation.astype(jnp.float32) * (1.0 / 65536.0)
    height = 1.0 - (2 * number + 1).astype(jnp.float32) / NDIR
    radial = jnp.sqrt(jnp.maximum(1.0 - height * height, 0.0))
    return radial * cos_turns(part), radial * cos_turns(part - 0.25), height


def kernel(sizes, cell_area, points, density, incident, precond, receivers, out,
           pbuf, w0buf, wbuf, wlast, table, plane, cols, toward, w0out, dloc, iloc, ploc, rloc, dpart, ipart, ppart,
           state, inc, inv, swap_out, swap_in,
           lsem, psend, w0send, wsend, lsend, prcv, w0rcv, wrcv, lrcv, xsend, xrcv):
    density_out, far_out = out.at[0], out.at[1]
    T, S = sizes
    n = T * S
    g, tz, sx, c = (lax.axis_index(a) for a in AXES)
    q = tz * S + sx
    me = 2 * q + c
    other = 1 - c

    def near(j):
        if unroll and isinstance(j, int):
            return dests[j]
        return nearest(jnp.int32(j))

    def nearest(j):
        k, b = lax.div(j, S), lax.rem(j, S)
        inner = jnp.minimum(tz, T - 1 - tz)
        alternating = tz + lax.div(k + 1, 2) * (2 * lax.rem(k, 2) - 1)
        tail = jnp.where(tz <= T - 1 - tz, k, T - 1 - k)
        z = jnp.where(k <= 2 * inner, alternating, tail)
        x = lax.rem(sx + b, S)
        return z, x

    def chip(j):
        z, x = near(j)
        return z * S + x

    unroll = n <= 8
    dests = [nearest(jnp.int32(j)) for j in range(n)] if unroll else []

    def each(start, stop, body):
        if unroll:
            for j in range(start, stop):
                body(j)
        else:
            lax.fori_loop(start, stop, lambda j, z: (body(j), z)[1], 0)

    def sums_of(step, total):
        if unroll:
            for j in range(1, n):
                total = step(j, total)
            return total
        return lax.fori_loop(1, n, step, total)

    loads = [
        pltpu.make_async_copy(points, pbuf.at[me], lsem.at[0]),
        pltpu.make_async_copy(density, dloc, lsem.at[1]),
        pltpu.make_async_copy(incident, iloc, lsem.at[2]),
        pltpu.make_async_copy(precond, ploc, lsem.at[3]),
        pltpu.make_async_copy(receivers.at[me], rloc, lsem.at[4]),
    ]
    for load in loads:
        load.start()

    barrier = pltpu.get_barrier_semaphore()

    def greet(i):
        z, x = near(n - 1 - i)
        for s in range(2):
            pl.semaphore_signal(barrier, inc=1, device_id=(g, z, x, s), device_id_type=MESH)

    each(0, n - 1, greet)
    pl.semaphore_signal(barrier, inc=1, device_id=(g, tz, sx, other), device_id_type=MESH)

    for load in loads:
        load.wait()
    w0 = (dloc[...] * cell_area).astype(jnp.bfloat16)
    w0out[...] = w0
    w0buf[me] = w0out[c]
    pl.semaphore_wait(barrier, 2 * n - 1)

    def first_copy(kind, z, x, s, slot):
        source, target, send, receive = (
            (pbuf.at[me], pbuf.at[me], psend, prcv), (w0out.at[s], w0buf.at[me], w0send, w0rcv))[kind]
        return pltpu.make_async_remote_copy(
            source, target, send.at[slot], receive.at[me], device_id=(g, z, x, s), device_id_type=MESH)

    def start_first(kind, i):
        j = i + 1
        z, x = near(j)
        for s in range(2):
            first_copy(kind, z, x, s, 2 * j + s).start()

    for kind in range(2):
        first_copy(kind, tz, sx, other, 0).start()
        each(0, n - 1, functools.partial(start_first, kind))
    swaps = [
        pltpu.make_async_remote_copy(
            source, target, xsend.at[i], xrcv.at[i], device_id=(g, tz, sx, other), device_id_type=MESH)
        for i, (source, target) in enumerate((
            (dloc.at[other], dpart), (iloc.at[other], ipart), (ploc, ppart)))
    ]
    for copy in swaps:
        copy.start()

    def wait_first(buffer, semaphore, index):
        pltpu.make_async_copy(buffer.at[index], buffer.at[index], semaphore.at[index]).wait()

    def spread(store, half, rows):
        for axis in range(3):
            row = jnp.broadcast_to(rows[axis], (LANES, LANES))
            store[axis, half * LANES:(half + 1) * LANES, :] = row.T

    def build(store, maker, targets, index, scale):
        sources = [pbuf[index + h] * scale for h in range(2)]
        for start in range(0, store.shape[0], CHUNK):
            left = [targets[a, start:start + CHUNK, :] for a in range(3)]
            for h in range(2):
                value = maker(left, [sources[h][a:a + 1, :] for a in range(3)])
                store[start:start + CHUNK, h * LANES:(h + 1) * LANES] = value.astype(jnp.bfloat16)

    def single_layer(targets, sources):
        dx, dy, dz = (t - s for t, s in zip(targets, sources))
        squared = dx * dx + dy * dy + dz * dz
        turns = squared * lax.rsqrt(jnp.maximum(squared, 1e-30))
        return cos_turns(turns, TURNS / FOUR_PI) * lax.rsqrt(squared + (TURNS * SMOOTHING) ** 2)

    def far_kernel(directed, sources):
        turns = directed[0] * sources[0] + directed[1] * sources[1] + directed[2] * sources[2]
        return cos_turns(turns)

    def product(left, right):
        return lax.dot_general(left, right, (((1,), (1,)), ((), ())), preferred_element_type=jnp.float32)

    def ordered(mine, partner):
        first = c == 0
        return jnp.concatenate(
            [jnp.where(first, mine, partner), jnp.where(first, partner, mine)], axis=-1)

    toward_rows = directions(rloc[...])
    spread(toward, 0, [row * TURNS for row in toward_rows])
    wait_first(pbuf, prcv, 2 * q + other)
    for half in range(2):
        spread(cols, half, [pbuf[2 * q + half][a:a + 1] * TURNS for a in range(3)])
    build(table.at[0], single_layer, cols, 2 * q, TURNS)
    for copy in swaps:
        copy.wait_recv()
    state[...] = ordered(dloc[c], dpart[...])
    inc[...] = ordered(iloc[c], ipart[...])
    inv[...] = 1.0 / ordered(ploc[...], ppart[...])

    def table_step(j, carry):
        index = 2 * chip(j)
        wait_first(pbuf, prcv, index)
        wait_first(pbuf, prcv, index + 1)
        build(table.at[j], single_layer, cols, index, TURNS)
        return carry

    def first_product(j, total):
        index = 2 * chip(j)
        weighted = jnp.concatenate([w0buf[index], w0buf[index + 1]], axis=1)
        return total + product(weighted, table[j])

    def first_step(j, total):
        index = 2 * chip(j)
        wait_first(w0buf, w0rcv, index)
        wait_first(w0buf, w0rcv, index + 1)
        return first_product(j, total)

    wait_first(w0buf, w0rcv, 2 * q + other)
    lax.fori_loop(1, n, table_step, 0)
    field = first_product(jnp.int32(0), jnp.zeros((w0out.shape[1], 2 * LANES), jnp.float32))
    field = sums_of(first_step, field)

    def last_copy(z, x, s):
        block = wlast.at[c * n + q]
        return pltpu.make_async_remote_copy(
            block, block, lsend, lrcv.at[c * n + q], device_id=(g, z, x, s), device_id_type=MESH)

    def send_last(cores, i):
        z, x = near(n - 1 - i)
        for s in cores:
            last_copy(z, x, s).start()

    def update(r, total):
        fresh = state[...] - (total + inc[...]) * inv[...]
        weighted = (fresh * cell_area).astype(jnp.bfloat16)
        if r == ITERS - 1:
            wlast[c * n + q] = weighted
            each(0, n - 1, functools.partial(send_last, [0, 1]))
            last_copy(tz, sx, other).start()
            return fresh
        state[...] = fresh
        wbuf[r, q] = weighted

        def send(i):
            z, x = near(n - 1 - i)
            pltpu.make_async_remote_copy(
                wbuf.at[r, q], wbuf.at[r, q], wsend.at[r], wrcv.at[r % 2, q],
                device_id=(g, z, x, c), device_id_type=MESH).start()

        each(0, n - 1, send)
        return fresh

    def plane_step(j, carry):
        index = 2 * chip(j)
        build(plane.at[j], far_kernel, toward, index, 1.0)
        return carry

    def gathered(r):
        def step(j, sums):
            index = chip(j)
            slot = wbuf.at[r, index]
            pltpu.make_async_copy(slot, slot, wrcv.at[r % 2, index]).wait()
            return sums + product(wbuf[r, index], table[j])

        return sums_of(step, product(wbuf[r, q], table[0]))

    def last_wait(index):
        pltpu.make_async_copy(wlast.at[index], wlast.at[index], lrcv.at[index]).wait()

    def far_product(j):
        index = chip(j)
        return product(jnp.concatenate([wlast[index], wlast[n + index]], axis=0), plane[j])

    def far_step(j, sums):
        for s in range(2):
            last_wait(s * n + chip(j))
        return sums + far_product(j)

    share = -(-n // ITERS)
    for r in range(ITERS):
        fresh = update(r, field)
        last = r == ITERS - 1
        if last:
            low, high = fresh[:, :LANES], fresh[:, LANES:]
            swap_out[0] = jnp.where(c == 0, high, low)
            density_out[c] = jnp.where(c == 0, low, high)
            dswap = pltpu.make_async_remote_copy(
                swap_out.at[0], swap_in.at[0], xsend.at[3], xrcv.at[3],
                device_id=(g, tz, sx, other), device_id_type=MESH)
            dswap.start()
        lax.fori_loop(min(r * share, n), min((r + 1) * share, n), plane_step, 0)
        if last:
            dswap.wait_recv()
            density_out[other] = swap_in[0]
            continue
        field = gathered(r)

    def end_first(i):
        z, x = near(i)
        for s in range(2):
            for kind in range(2):
                first_copy(kind, z, x, s, 2 * i + s).wait_send()

    each(1, n, end_first)
    for kind in range(2):
        first_copy(kind, tz, sx, other, 0).wait_send()
    for r in range(ITERS - 1):
        sent = wbuf.at[r, pl.ds(0, n - 1)]
        pltpu.make_async_copy(sent, sent, wsend.at[r]).wait()
    for copy in swaps:
        copy.wait_send()
    dswap.wait_send()

    last_wait(other * n + q)
    far = sums_of(far_step, far_product(0))
    half = far_out.shape[1]
    far_out[0] = far[:half]
    far_out[1] = far[half:]

    sent = wlast.at[pl.ds(0, 2 * n - 1)]
    pltpu.make_async_copy(sent, sent, lsend).wait()


def shards(points, density, incident, precond, receivers):
    T, S = lax.axis_size("tgt"), lax.axis_size("src")
    n = T * S
    columns, own = density.shape
    half = columns // 2
    f32, bf16 = jnp.float32, jnp.bfloat16
    cell_area = FOUR_PI / (own * n * 2)
    block = pltpu.VMEM((2, 2, half, own), f32)
    anywhere = pl.BlockSpec(memory_space=pl.ANY)
    vmem = pl.BlockSpec(memory_space=pltpu.VMEM)
    dma = pltpu.SemaphoreType.DMA
    out = pl.pallas_call(
        functools.partial(kernel, (T, S), cell_area),
        out_shape=block,
        in_specs=[anywhere] * 5,
        out_specs=vmem,
        scratch_shapes=[
            pltpu.VMEM((2 * n, 3, own), f32),
            pltpu.VMEM((2 * n, half, own), bf16),
            pltpu.VMEM((ITERS - 1, n, half, 2 * own), bf16),
            pltpu.VMEM((2 * n, half, 2 * own), bf16),
            pltpu.VMEM((n, 2 * own, 2 * own), bf16),
            pltpu.VMEM((n, own, 2 * own), bf16),
            pltpu.VMEM((3, 2 * own, own), f32),
            pltpu.VMEM((3, own, own), f32),
            pltpu.VMEM((2, half, own), bf16),
            pltpu.VMEM((2, half, own), f32),
            pltpu.VMEM((2, half, own), f32),
            pltpu.VMEM((1, own), f32),
            pltpu.VMEM((1, own), jnp.int32),
            pltpu.VMEM((half, own), f32),
            pltpu.VMEM((half, own), f32),
            pltpu.VMEM((1, own), f32),
            pltpu.VMEM((half, 2 * own), f32),
            pltpu.VMEM((half, 2 * own), f32),
            pltpu.VMEM((1, 2 * own), f32),
            pltpu.VMEM((1, half, own), f32),
            pltpu.VMEM((1, half, own), f32),
            dma((5,)),
            dma((2 * n,)),
            dma((2 * n,)),
            dma((ITERS - 1,)),
            dma(()),
            dma((2 * n,)),
            dma((2 * n,)),
            dma((2, n)),
            dma((2 * n,)),
            dma((4,)),
            dma((4,)),
        ],
        compiler_params=pltpu.CompilerParams(
            collective_id=0, has_side_effects=True, vmem_limit_bytes=60 * 1024 * 1024),
    )(
        points,
        density.reshape(2, half, own),
        incident.reshape(2, half, own),
        precond.reshape(1, own),
        receivers.reshape(2 * n, 1, own),
    )
    return out[0].reshape(columns, own), out[1].reshape(columns, own)


def solution(mesh):
    split = P(None, AXES)
    return jax.shard_map(
        shards,
        mesh=mesh,
        in_specs=(split, split, split, P(AXES), P("groups")),
        out_specs=(split, split),
        check_vma=False,
    )
```

profile of v0, /device:TPU:0, one launch (start us, length us, event | category | flops | bytes accessed | tf_op | source)
XLA Modules:
  0.0 30.2 jit_solution(9822348244936108474)
XLA Ops:
  0.6 28.9 %shard_map.68 = f32[2,2,16,128]{3,2,1,0:T(8,128)S(1)} custom-call(f32[3,128]{1,0:T(4,128)} %points.1, f32[2,16,128]{2,1,0:T(8,128)} %bitcast.6, f32[2,16,128]{2,1,0:T(8,128)} %bitcast.7, f32[1,128]{1,0:T(1,128)} %bitcast.11, s32[16,1,128]{2,1,0:T(1,128)} %bitcast.10), custom_call_target="tpu_custom_call" | custom-call | tf_op jit(solution)/shard_map/pallas_call | solution.py:332
  29.5 0.6 %fusion = (f32[1,2,16,128]{3,2,1,0:T(8,128)}, f32[1,2,16,128]{3,2,1,0:T(8,128)}) fusion(f32[2,2,16,128]{3,2,1,0:T(8,128)S(1)} %shard_map.68), kind=kLoop, calls=%fused_computation | loop fusion | bytes 65536 | tf_op jit(solution)/shard_map/slice | solution.py:380
where the time goes:
time: 30.3 us; the launch traced here: 30.2 us
  Pallas kernels  28.9 us (95%)
  between operations  0.64 us (2%)
  local copies, waits for them, and re-layouts  0.61 us (2%)
    pallas_call x1, Pallas kernels, shards(): pl.pallas_call(functools.partial(kernel, (T, S), cell_area), out_shape=bl...  28.9 us
    slice x1, local copies, waits for them, and re-layouts, shards(): return (out[0].reshape(columns, own), out[1].reshape(columns, own))  0.61 us

commit v1 on v0

--- a/solution.py
+++ b/solution.py
@@ -318,6 +318,345 @@
     pltpu.make_async_copy(sent, sent, lsend).wait()
 
 
+FOLD = np.polynomial.chebyshev.Chebyshev.interpolate(
+    lambda v: -np.sin(2.0 * np.pi * np.sqrt(v)) / np.sqrt(v), 3, domain=[0.0, 0.0625]
+).convert(kind=np.polynomial.Polynomial).coef
+FOLD = [float(c) for c in FOLD]
+MONIC = [c / FOLD[3] for c in FOLD[:3]]
+KAPPA = (FOUR_PI / (FOLD[3] * TURNS)) ** 2
+SOFT = (TURNS * SMOOTHING) ** 2
+DEPTH = 32
+
+
+def folded(turns):
+    g = jnp.abs(turns - jnp.round(turns)) - 0.25
+    return g, g * g
+
+
+def parts_of(value):
+    high = value.astype(jnp.bfloat16).astype(jnp.float32)
+    rest = value - high
+    middle = rest.astype(jnp.bfloat16).astype(jnp.float32)
+    return high, middle, rest - middle
+
+
+def stacked(groups):
+    return jnp.concatenate(groups + [jnp.zeros_like(groups[0])] * (DEPTH // 4 - len(groups)), axis=0)
+
+
+def column_kernel(sizes, cell_area, points, density, incident, precond, receivers, out,
+                  xloc, dloc, iloc, ploc, rloc, pmsg, pbuf, dmsg, dbuf, left, right, aim, table, plane,
+                  state, inc, inv, wfin, wall, dsend, drcv,
+                  lsem, psend, prcv, dsnd, drv, tsend, trcv, wsend, wrcv, osend, orcv):
+    density_out, far_out = out.at[0], out.at[1]
+    T, S = sizes
+    n = T * S
+    D = 2 * n
+    wide = 2 * LANES
+    share = dloc.shape[0] // D
+    f32, bf16 = jnp.float32, jnp.bfloat16
+    g, tz, sx, c = (lax.axis_index(a) for a in AXES)
+    q = tz * S + sx
+    me = 2 * q + c
+    other = 1 - c
+
+    def nearest(j):
+        k, b = lax.div(j, S), lax.rem(j, S)
+        inner = jnp.minimum(tz, T - 1 - tz)
+        alternating = tz + lax.div(k + 1, 2) * (2 * lax.rem(k, 2) - 1)
+        tail = jnp.where(tz <= T - 1 - tz, k, T - 1 - k)
+        z = jnp.where(k <= 2 * inner, alternating, tail)
+        x = lax.rem(sx + b, S)
+        return z, x
+
+    dests = [nearest(jnp.int32(j)) for j in range(n)]
+
+    def chip(j):
+        z, x = dests[j] if isinstance(j, int) else nearest(j)
+        return z * S + x
+
+    peers = [(dests[j], s) for j in range(1, n) for s in range(2)]
+    sibling = (dests[0], other)
+
+    def place(peer):
+        (z, x), s = peer
+        return (g, z, x, s)
+
+    def index_of(peer):
+        (z, x), s = peer
+        return 2 * (z * S + x) + s
+
+    loads = [
+        pltpu.make_async_copy(points, xloc, lsem.at[0]),
+        pltpu.make_async_copy(precond, ploc, lsem.at[1]),
+        pltpu.make_async_copy(density, dloc, lsem.at[2]),
+        pltpu.make_async_copy(incident, iloc, lsem.at[3]),
+        pltpu.make_async_copy(receivers.at[me], rloc, lsem.at[4]),
+    ]
+    for load in loads:
+        load.start()
+    barrier = pltpu.get_barrier_semaphore()
+    for peer in peers[::-1] + [sibling]:
+        pl.semaphore_signal(barrier, inc=1, device_id=place(peer), device_id_type=MESH)
+    for load in loads:
+        load.wait()
+    message = jnp.concatenate([xloc[...], 1.0 / ploc[...]], axis=0)
+    pmsg[...] = message
+    pbuf[me] = message
+    for e in range(D):
+        rows = slice(share * e, share * (e + 1))
+        dmsg[e] = jnp.concatenate([dloc[rows, :], iloc[rows, :]], axis=0)
+    dbuf[me] = dmsg[me]
+    pl.semaphore_wait(barrier, D - 1)
+
+    def send(source, target, send_sem, receive_sem, peer):
+        pltpu.make_async_remote_copy(
+            source, target, send_sem, receive_sem, device_id=place(peer), device_id_type=MESH).start()
+
+    def await_in(target, semaphore):
+        pltpu.make_async_copy(target, target, semaphore).wait()
+
+    for peer in [sibling] + peers:
+        send(pmsg, pbuf.at[me], psend, prcv.at[me], peer)
+    for peer in [sibling] + peers:
+        send(dmsg.at[index_of(peer)], dbuf.at[me], dsnd, drv.at[me], peer)
+
+    row4 = lax.broadcasted_iota(jnp.int32, (4, wide), 0)
+    coordinate = row4 < 3
+
+    def product(a, b):
+        return lax.dot_general(a, b, (((1,), (0,)), ((), ())), preferred_element_type=f32)
+
+    def features(j):
+        index = 2 * chip(j)
+        x = jnp.concatenate([pbuf[index], pbuf[index + 1]], axis=1) * TURNS
+        squares = x * x
+        a = squares[0:1] + squares[1:2] + squares[2:3]
+        high, middle, low = parts_of(jnp.where(coordinate, x, a))
+        scale = jnp.where(coordinate, -2.0, 1.0)
+        high, middle, low = high * scale, middle * scale, low * scale
+        ones = jnp.where(coordinate, 1.0, 0.0)
+        left[j] = stacked([high, high, high, middle, middle, low, ones]).T.astype(bf16)
+        for h, (factor, shift) in enumerate(((1.0, 0.0), (KAPPA, KAPPA * SOFT))):
+            high, middle, low = parts_of(jnp.where(coordinate, x, 1.0) * factor)
+            tail = jnp.concatenate(list(parts_of(a * factor + shift)) + [jnp.zeros_like(a)], axis=0)
+            right[j, :, h * wide:(h + 1) * wide] = stacked(
+                [high, middle, low, high, middle, high, tail]).astype(bf16)
+
+    def entries(pair, diagonal):
+        squared, softened = pair[:, :wide], pair[:, wide:]
+        if diagonal is not None:
+            squared = jnp.where(diagonal, 0.0, squared)
+            softened = jnp.where(diagonal, KAPPA * SOFT, softened)
+        turns = squared * lax.rsqrt(jnp.maximum(squared, 1e-30))
+        fold, v = folded(turns)
+        total = ((v + MONIC[2]) * v + MONIC[1]) * v + MONIC[0]
+        return (total * fold * lax.rsqrt(softened)).astype(bf16)
+
+    def build(a, blocks):
+        for start in range(0, wide, LANES):
+            rows = slice(start, start + LANES)
+            for b, mirror in blocks:
+                diagonal = None
+                if not mirror:
+                    shape = (LANES, wide)
+                    diagonal = lax.broadcasted_iota(jnp.int32, shape, 0) + start == lax.broadcasted_iota(jnp.int32, shape, 1)
+                value = entries(product(left[a, rows, :], right[b]), diagonal)
+                table[a, b, rows, :] = value
+                if mirror:
+                    table[b, a, :, rows] = value.T
+
+    def swap(k, m):
+        row = 2 * k + c
+        block = table.at[row, pl.ds(2 * m, 2)]
+        return pltpu.make_async_remote_copy(
+            block, block, tsend.at[k, m], trcv.at[k, m], device_id=place(sibling), device_id_type=MESH)
+
+    def swap_own(k):
+        row = 2 * k + c
+        block = table.at[row, row]
+        return pltpu.make_async_remote_copy(
+            block, block, tsend.at[k, k], trcv.at[k, k], device_id=place(sibling), device_id_type=MESH)
+
+    rows3 = directions(rloc[...])
+    aims = jnp.concatenate(list(rows3) + [jnp.zeros_like(rows3[0])], axis=0) * -0.5
+    high, middle, low = parts_of(aims)
+    aim[...] = stacked([high, middle, low, high, middle, high]).astype(bf16)
+
+    def step(k, carry):
+        for h in range(2):
+            j = 2 * k + h
+            index = 2 * chip(j)
+            for s in range(2):
+                @pl.when(index + s != me)
+                def _():
+                    await_in(pbuf.at[index + s], prcv.at[index + s])
+            features(j)
+
+        def across(m, z):
+            build(2 * k + c, [(2 * m, True), (2 * m + 1, True)])
+            swap(k, m).start()
+            return z
+
+        lax.fori_loop(0, k, across, 0)
+        build(2 * k + c, [(2 * k + c, False)])
+        swap_own(k).start()
+        build(2 * k + 1, [(2 * k, True)])
+        return carry
+
+    lax.fori_loop(0, n // 2, step, 0)
+
+    state[...] = jnp.zeros_like(state)
+    inc[...] = jnp.zeros_like(inc)
+    inv[...] = jnp.zeros_like(inv)
+    for j in range(n):
+        index = 2 * chip(j)
+        for s in range(2):
+            lanes = slice((2 * j + s) * LANES, (2 * j + s + 1) * LANES)
+            if j > 0:
+                await_in(dbuf.at[index + s], drv.at[index + s])
+            elif s == 0:
+                await_in(dbuf.at[2 * q + other], drv.at[2 * q + other])
+            message = dbuf[index + s]
+            state[0:share, lanes] = message[:share]
+            inc[0:share, lanes] = message[share:]
+            inv[0:share, lanes] = jnp.broadcast_to(pbuf[index + s][3:4], (share, LANES))
+
+    def mirror_step(k, carry):
+        row = 2 * k + other
+
+        def one(m, z):
+            await_in(table.at[row, pl.ds(2 * m, 2)], trcv.at[k, m])
+            for h in range(2):
+                table[2 * m + h, row] = table[row, 2 * m + h].T
+            return z
+
+        lax.fori_loop(0, k, one, 0)
+        await_in(table.at[row, row], trcv.at[k, k])
+        return carry
+
+    lax.fori_loop(0, n // 2, mirror_step, 0)
+
+    def iterate(r, carry):
+        weighted = (state[...] * cell_area).astype(bf16)
+        for b in range(n):
+            lanes = slice(b * wide, (b + 1) * wide)
+            field = product(weighted[:, :wide], table[0, b])
+            for a in range(1, n):
+                field = field + product(weighted[:, a * wide:(a + 1) * wide], table[a, b])
+            state[:, lanes] = state[:, lanes] - (field + inc[:, lanes]) * inv[:, lanes]
+        return carry
+
+    lax.fori_loop(0, ITERS, iterate, 0)
+
+    weighted = (state[...] * cell_area).astype(bf16)
+    for j in range(n):
+        wfin[chip(j)] = weighted[0:share, j * wide:(j + 1) * wide]
+    for peer in peers[::-1] + [sibling]:
+        send(wfin, wall.at[me], wsend, wrcv.at[me], peer)
+    for j in range(n):
+        for s in range(2):
+            dsend[2 * chip(j) + s] = state[0:share, (2 * j + s) * LANES:(2 * j + s + 1) * LANES]
+    for peer in peers[::-1] + [sibling]:
+        send(dsend.at[index_of(peer)], drcv.at[me], osend, orcv.at[me], peer)
+    wall[me] = wfin[...]
+    drcv[me] = dsend[me]
+
+    def plane_step(j, carry):
+        fold, v = folded(product(left[j], aim[...]))
+        total = ((FOLD[3] * v + FOLD[2]) * v + FOLD[1]) * v + FOLD[0]
+        plane[j] = (total * fold).astype(bf16)
+        return carry
+
+    lax.fori_loop(0, n, plane_step, 0)
+
+    def finish_sends():
+        for k in range(n // 2):
+            for m in range(k):
+                swap(k, m).wait_send()
+            swap_own(k).wait_send()
+        await_in(pbuf.at[pl.ds(0, D - 1)], psend)
+        await_in(dbuf.at[pl.ds(0, D - 1)], dsnd)
+
+    finish_sends()
+    for peer in [sibling] + peers:
+        index = index_of(peer)
+        await_in(wall.at[index], wrcv.at[index])
+    for j in range(n):
+        index = chip(j)
+        gathered = jnp.concatenate([wall[d, index].astype(f32) for d in range(D)], axis=0).astype(bf16)
+        part = product(gathered, plane[j])
+        far = part if j == 0 else far + part
+    half = far_out.shape[1]
+    far_out[0] = far[:half]
+    far_out[1] = far[half:]
+    for peer in [sibling] + peers:
+        index = index_of(peer)
+        await_in(drcv.at[index], orcv.at[index])
+    whole = jnp.concatenate([drcv[d] for d in range(D)], axis=0)
+    density_out[0] = whole[:half]
+    density_out[1] = whole[half:]
+    await_in(wall.at[pl.ds(0, D - 1)], wsend)
+    await_in(drcv.at[pl.ds(0, D - 1)], osend)
+
+
+def column_call(sizes, cell_area, points, density, incident, precond, receivers):
+    T, S = sizes
+    n = T * S
+    D = 2 * n
+    columns, own = density.shape
+    half = columns // 2
+    share = columns // D
+    wide = 2 * own
+    f32, bf16 = jnp.float32, jnp.bfloat16
+    anywhere = pl.BlockSpec(memory_space=pl.ANY)
+    dma = pltpu.SemaphoreType.DMA
+    return pl.pallas_call(
+        functools.partial(column_kernel, sizes, cell_area),
+        out_shape=jax.ShapeDtypeStruct((2, 2, half, own), f32),
+        in_specs=[anywhere] * 5,
+        out_specs=pl.BlockSpec(memory_space=pltpu.VMEM),
+        scratch_shapes=[
+            pltpu.VMEM((3, own), f32),
+            pltpu.VMEM((columns, own), f32),
+            pltpu.VMEM((columns, own), f32),
+            pltpu.VMEM((1, own), f32),
+            pltpu.VMEM((1, own), jnp.int32),
+            pltpu.VMEM((4, own), f32),
+            pltpu.VMEM((D, 4, own), f32),
+            pltpu.VMEM((D, 2 * share, own), f32),
+            pltpu.VMEM((D, 2 * share, own), f32),
+            pltpu.VMEM((n, wide, DEPTH), bf16),
+            pltpu.VMEM((n, DEPTH, 2 * wide), bf16),
+            pltpu.VMEM((DEPTH, own), bf16),
+            pltpu.VMEM((n, n, wide, wide), bf16),
+            pltpu.VMEM((n, wide, own), bf16),
+            pltpu.VMEM((8, n * wide), f32),
+            pltpu.VMEM((8, n * wide), f32),
+            pltpu.VMEM((8, n * wide), f32),
+            pltpu.VMEM((n, share, wide), bf16),
+            pltpu.VMEM((D, n, share, wide), bf16),
+            pltpu.VMEM((D, share, own), f32),
+            pltpu.VMEM((D, share, own), f32),
+            dma((5,)),
+            dma(()),
+            dma((D,)),
+            dma(()),
+            dma((D,)),
+            dma((n // 2, n // 2)),
+            dma((n // 2, n // 2)),
+            dma(()),
+            dma((D,)),
+            dma(()),
+            dma((D,)),
+        ],
+        compiler_params=pltpu.CompilerParams(
+            collective_id=0, has_side_effects=True, vmem_limit_bytes=60 * 1024 * 1024),
+    )(
+        points, density, incident, precond.reshape(1, own), receivers.reshape(D, 1, own),
+    )
+
+
 def shards(points, density, incident, precond, receivers):
     T, S = lax.axis_size("tgt"), lax.axis_size("src")
     n = T * S
@@ -325,6 +664,9 @@
     half = columns // 2
     f32, bf16 = jnp.float32, jnp.bfloat16
     cell_area = FOUR_PI / (own * n * 2)
+    if n <= 8 and n % 2 == 0 and columns == 4 * n and own == LANES:
+        out = column_call((T, S), cell_area, points, density, incident, precond, receivers)
+        return out[0].reshape(columns, own), out[1].reshape(columns, own)
     block = pltpu.VMEM((2, 2, half, own), f32)
     anywhere = pl.BlockSpec(memory_space=pl.ANY)
     vmem = pl.BlockSpec(memory_space=pltpu.VMEM)

time: 30.3 us -> 30.2 us (level)
  Pallas kernels: 28.9 us -> 28 us
  local copies, waits for them, and re-layouts: 0.61 us -> 1.35 us
    pallas_call x1, Pallas kernels: 28.9 us -> 28 us  [column_call(): pl.pallas_call(functools.partial(column_kernel, sizes, cell_area), out_sh...]
    slice x1, local copies, waits for them, and re-layouts: 0.61 us -> 1.35 us  [shards(): return (out[0].reshape(columns, own), out[1].reshape(columns, own))]
where the time goes in v1:
time: 30.2 us; the launch traced here: 30 us
  Pallas kernels  28 us (93%)
  local copies, waits for them, and re-layouts  1.35 us (4%)
  between operations  0.64 us (2%)
    pallas_call x1, Pallas kernels, column_call(): pl.pallas_call(functools.partial(column_kernel, sizes, cell_area), out_sh...  28 us
    slice x1, local copies, waits for them, and re-layouts, shards(): return (out[0].reshape(columns, own), out[1].reshape(columns, own))  1.35 us

profile of v1, /device:TPU:0, one launch (start us, length us, event | category | flops | bytes accessed | tf_op | source)
XLA Modules:
  0.0 30.0 jit_solution(18038443063690981697)
XLA Ops:
  0.6 28.0 %shard_map.68 = f32[2,2,16,128]{3,2,1,0:T(8,128)} custom-call(f32[3,128]{1,0:T(4,128)} %points.1, f32[32,128]{1,0:T(8,128)} %density.1, f32[32,128]{1,0:T(8,128)} %incident.1, f32[1,128]{1,0:T(1,128)} %bitcast.7, s32[16,1,128]{2,1,0:T(1,128)} %bitcast.6), custom_call_target="tpu_custom_call" | custom-call | tf_op jit(solution)/shard_map/pallas_call | solution.py:614
  28.6 1.3 %fusion = (f32[1,2,16,128]{3,2,1,0:T(8,128)}, f32[1,2,16,128]{3,2,1,0:T(8,128)}) fusion(f32[2,2,16,128]{3,2,1,0:T(8,128)} %shard_map.68), kind=kLoop, calls=%fused_computation | loop fusion | bytes 65536 | tf_op jit(solution)/shard_map/slice | solution.py:669

commit v2 on v1

--- a/solution.py
+++ b/solution.py
@@ -326,6 +326,7 @@
 KAPPA = (FOUR_PI / (FOLD[3] * TURNS)) ** 2
 SOFT = (TURNS * SMOOTHING) ** 2
 DEPTH = 32
+ROWS = 64
 
 
 def folded(turns):
@@ -345,7 +346,7 @@
 
 
 def column_kernel(sizes, cell_area, points, density, incident, precond, receivers, out,
-                  xloc, dloc, iloc, ploc, rloc, pmsg, pbuf, dmsg, dbuf, left, right, aim, table, plane,
+                  xloc, dloc, iloc, ploc, rloc, pmsg, pbuf, dmsg, dbuf, left, right, aim, stage, table, plane,
                   state, inc, inv, wfin, wall, dsend, drcv,
                   lsem, psend, prcv, dsnd, drv, tsend, trcv, wsend, wrcv, osend, orcv):
     density_out, far_out = out.at[0], out.at[1]
@@ -371,9 +372,11 @@
 
     dests = [nearest(jnp.int32(j)) for j in range(n)]
 
-    def chip(j):
-        z, x = dests[j] if isinstance(j, int) else nearest(j)
-        return z * S + x
+    spots = []
+    for k in range(n // 2):
+        for h in (c, other):
+            z, x = nearest(2 * k + h)
+            spots.append(z * S + x)
 
     peers = [(dests[j], s) for j in range(1, n) for s in range(2)]
     sibling = (dests[0], other)
@@ -417,9 +420,9 @@
         pltpu.make_async_copy(target, target, semaphore).wait()
 
     for peer in [sibling] + peers:
-        send(pmsg, pbuf.at[me], psend, prcv.at[me], peer)
+        send(pmsg, pbuf.at[me], psend, prcv.at[tz], peer)
     for peer in [sibling] + peers:
-        send(dmsg.at[index_of(peer)], dbuf.at[me], dsnd, drv.at[me], peer)
+        send(dmsg.at[index_of(peer)], dbuf.at[me], dsnd, drv, peer)
 
     row4 = lax.broadcasted_iota(jnp.int32, (4, wide), 0)
     coordinate = row4 < 3
@@ -427,8 +430,8 @@
     def product(a, b):
         return lax.dot_general(a, b, (((1,), (0,)), ((), ())), preferred_element_type=f32)
 
-    def features(j):
-        index = 2 * chip(j)
+    def features(p):
+        index = 2 * spots[p]
         x = jnp.concatenate([pbuf[index], pbuf[index + 1]], axis=1) * TURNS
         squares = x * x
         a = squares[0:1] + squares[1:2] + squares[2:3]
@@ -436,11 +439,11 @@
         scale = jnp.where(coordinate, -2.0, 1.0)
         high, middle, low = high * scale, middle * scale, low * scale
         ones = jnp.where(coordinate, 1.0, 0.0)
-        left[j] = stacked([high, high, high, middle, middle, low, ones]).T.astype(bf16)
+        left[p] = stacked([high, high, high, middle, middle, low, ones]).T.astype(bf16)
         for h, (factor, shift) in enumerate(((1.0, 0.0), (KAPPA, KAPPA * SOFT))):
             high, middle, low = parts_of(jnp.where(coordinate, x, 1.0) * factor)
             tail = jnp.concatenate(list(parts_of(a * factor + shift)) + [jnp.zeros_like(a)], axis=0)
-            right[j, :, h * wide:(h + 1) * wide] = stacked(
+            right[p, :, h * wide:(h + 1) * wide] = stacked(
                 [high, middle, low, high, middle, high, tail]).astype(bf16)
 
     def entries(pair, diagonal):
@@ -453,112 +456,127 @@
         total = ((v + MONIC[2]) * v + MONIC[1]) * v + MONIC[0]
         return (total * fold * lax.rsqrt(softened)).astype(bf16)
 
-    def build(a, blocks):
-        for start in range(0, wide, LANES):
-            rows = slice(start, start + LANES)
-            for b, mirror in blocks:
+    def distances(unit, slot):
+        for i, (a, b) in enumerate(unit):
+            stage[slot, i] = product(left[a], right[b])
+
+    def shade(unit, slot):
+        for start in range(0, wide, ROWS):
+            rows = slice(start, start + ROWS)
+            for i, (a, b) in enumerate(unit):
                 diagonal = None
-                if not mirror:
-                    shape = (LANES, wide)
+                if a == b:
+                    shape = (ROWS, wide)
                     diagonal = lax.broadcasted_iota(jnp.int32, shape, 0) + start == lax.broadcasted_iota(jnp.int32, shape, 1)
-                value = entries(product(left[a, rows, :], right[b]), diagonal)
-                table[a, b, rows, :] = value
-                if mirror:
-                    table[b, a, :, rows] = value.T
-
-    def swap(k, m):
-        row = 2 * k + c
-        block = table.at[row, pl.ds(2 * m, 2)]
+                table[a, b, rows, :] = entries(stage[slot, i, rows, :], diagonal)
+
+    def swap(k, b):
         return pltpu.make_async_remote_copy(
-            block, block, tsend.at[k, m], trcv.at[k, m], device_id=place(sibling), device_id_type=MESH)
-
-    def swap_own(k):
-        row = 2 * k + c
-        block = table.at[row, row]
-        return pltpu.make_async_remote_copy(
-            block, block, tsend.at[k, k], trcv.at[k, k], device_id=place(sibling), device_id_type=MESH)
+            table.at[2 * k, b], table.at[2 * k + 1, b ^ 1], tsend.at[k], trcv.at[k],
+            device_id=place(sibling), device_id_type=MESH)
+
+    def flip(a, b):
+        table[b, a] = table[a, b].T
+
+    def swapped(k):
+        return table.at[0, pl.ds(0, 2 * k + 1)]
 
     rows3 = directions(rloc[...])
     aims = jnp.concatenate(list(rows3) + [jnp.zeros_like(rows3[0])], axis=0) * -0.5
     high, middle, low = parts_of(aims)
     aim[...] = stacked([high, middle, low, high, middle, high]).astype(bf16)
 
-    def step(k, carry):
-        for h in range(2):
-            j = 2 * k + h
-            index = 2 * chip(j)
+    def plane_in(k):
+        count = 4 if k else 3
+        await_in(pbuf.at[pl.ds(0, count)], prcv.at[dests[2 * k][0]])
+        features(2 * k)
+        features(2 * k + 1)
+
+    def columns_in():
+        await_in(dbuf.at[pl.ds(0, D - 1)], drv)
+        state[...] = jnp.zeros_like(state)
+        inc[...] = jnp.zeros_like(inc)
+        inv[...] = jnp.zeros_like(inv)
+        for p in range(n):
             for s in range(2):
-                @pl.when(index + s != me)
-                def _():
-                    await_in(pbuf.at[index + s], prcv.at[index + s])
-            features(j)
-
-        def across(m, z):
-            build(2 * k + c, [(2 * m, True), (2 * m + 1, True)])
-            swap(k, m).start()
-            return z
-
-        lax.fori_loop(0, k, across, 0)
-        build(2 * k + c, [(2 * k + c, False)])
-        swap_own(k).start()
-        build(2 * k + 1, [(2 * k, True)])
-        return carry
-
-    lax.fori_loop(0, n // 2, step, 0)
-
-    state[...] = jnp.zeros_like(state)
-    inc[...] = jnp.zeros_like(inc)
-    inv[...] = jnp.zeros_like(inv)
-    for j in range(n):
-        index = 2 * chip(j)
-        for s in range(2):
-            lanes = slice((2 * j + s) * LANES, (2 * j + s + 1) * LANES)
-            if j > 0:
-                await_in(dbuf.at[index + s], drv.at[index + s])
-            elif s == 0:
-                await_in(dbuf.at[2 * q + other], drv.at[2 * q + other])
-            message = dbuf[index + s]
-            state[0:share, lanes] = message[:share]
-            inc[0:share, lanes] = message[share:]
-            inv[0:share, lanes] = jnp.broadcast_to(pbuf[index + s][3:4], (share, LANES))
-
-    def mirror_step(k, carry):
-        row = 2 * k + other
-
-        def one(m, z):
-            await_in(table.at[row, pl.ds(2 * m, 2)], trcv.at[k, m])
-            for h in range(2):
-                table[2 * m + h, row] = table[row, 2 * m + h].T
-            return z
-
-        lax.fori_loop(0, k, one, 0)
-        await_in(table.at[row, row], trcv.at[k, k])
-        return carry
-
-    lax.fori_loop(0, n // 2, mirror_step, 0)
+                index = 2 * spots[p] + s
+                lanes = slice((2 * p + s) * LANES, (2 * p + s + 1) * LANES)
+                message = dbuf[index]
+                state[0:share, lanes] = message[:share]
+                inc[0:share, lanes] = message[share:]
+                inv[0:share, lanes] = jnp.broadcast_to(pbuf[index][3:4], (share, LANES))
+
+    units = []
+    for k in range(n // 2):
+        units += [(k, [(2 * k, 2 * m), (2 * k, 2 * m + 1)]) for m in range(k)]
+        units += [(k, [(2 * k, 2 * k), (2 * k + 1, 2 * k)])]
+    last = n // 2 - 1
+    plane_in(0)
+    distances(units[0][1], 0)
+    flips = []
+    for i, (k, unit) in enumerate(units):
+        following = units[i + 1] if i + 1 < len(units) else None
+        if following and following[0] != k:
+            plane_in(following[0])
+        if unit[0][0] == unit[0][1]:
+            for old in [k - 1] if k else []:
+                await_in(swapped(old), trcv.at[old])
+                flips += [(2 * old + 1, b) for b in range(2 * old)]
+        for a, b in flips:
+            flip(a, b)
+        if following:
+            distances(following[1], (i + 1) % 2)
+        shade(unit, i % 2)
+        flips = [(a, b) for a, b in unit if a != b]
+        for a, b in unit:
+            if a == 2 * k:
+                swap(k, b).start()
+        if i == len(units) - 2:
+            columns_in()
+    for a, b in flips:
+        flip(a, b)
+
+    def piece(value, p):
+        return value[:, p * wide:(p + 1) * wide]
+
+    def gather_field(weighted, sources, b):
+        total = None
+        for a in sources:
+            part = product(piece(weighted, a), table[a, b])
+            total = part if total is None else total + part
+        return total
+
+    def update(field, b):
+        lanes = slice(b * wide, (b + 1) * wide)
+        state[:, lanes] = state[:, lanes] - (field + inc[:, lanes]) * inv[:, lanes]
+
+    weighted = (state[...] * cell_area).astype(bf16)
+    fields = [gather_field(weighted, range(n - 1), b) for b in range(n - 1)]
+    await_in(swapped(last), trcv.at[last])
+    for b in range(n - 2):
+        flip(n - 1, b)
+    for b in range(n - 1):
+        update(fields[b] + product(piece(weighted, n - 1), table[n - 1, b]), b)
+    update(gather_field(weighted, range(n), n - 1), n - 1)
 
     def iterate(r, carry):
         weighted = (state[...] * cell_area).astype(bf16)
         for b in range(n):
-            lanes = slice(b * wide, (b + 1) * wide)
-            field = product(weighted[:, :wide], table[0, b])
-            for a in range(1, n):
-                field = field + product(weighted[:, a * wide:(a + 1) * wide], table[a, b])
-            state[:, lanes] = state[:, lanes] - (field + inc[:, lanes]) * inv[:, lanes]
+            update(gather_field(weighted, range(n), b), b)
         return carry
 
-    lax.fori_loop(0, ITERS, iterate, 0)
+    lax.fori_loop(1, ITERS, iterate, 0)
 
     weighted = (state[...] * cell_area).astype(bf16)
-    for j in range(n):
-        wfin[chip(j)] = weighted[0:share, j * wide:(j + 1) * wide]
+    for p in range(n):
+        wfin[spots[p]] = weighted[0:share, p * wide:(p + 1) * wide]
     for peer in peers[::-1] + [sibling]:
-        send(wfin, wall.at[me], wsend, wrcv.at[me], peer)
-    for j in range(n):
+        send(wfin, wall.at[me], wsend, wrcv, peer)
+    for p in range(n):
         for s in range(2):
-            dsend[2 * chip(j) + s] = state[0:share, (2 * j + s) * LANES:(2 * j + s + 1) * LANES]
+            dsend[2 * spots[p] + s] = state[0:share, (2 * p + s) * LANES:(2 * p + s + 1) * LANES]
     for peer in peers[::-1] + [sibling]:
-        send(dsend.at[index_of(peer)], drcv.at[me], osend, orcv.at[me], peer)
+        send(dsend.at[index_of(peer)], drcv.at[me], osend, orcv, peer)
     wall[me] = wfin[...]
     drcv[me] = dsend[me]
 
@@ -572,27 +590,21 @@
 
     def finish_sends():
         for k in range(n // 2):
-            for m in range(k):
-                swap(k, m).wait_send()
-            swap_own(k).wait_send()
+            await_in(swapped(k), tsend.at[k])
         await_in(pbuf.at[pl.ds(0, D - 1)], psend)
         await_in(dbuf.at[pl.ds(0, D - 1)], dsnd)
 
     finish_sends()
-    for peer in [sibling] + peers:
-        index = index_of(peer)
-        await_in(wall.at[index], wrcv.at[index])
+    await_in(wall.at[pl.ds(0, D - 1)], wrcv)
     for j in range(n):
-        index = chip(j)
+        index = spots[j]
         gathered = jnp.concatenate([wall[d, index].astype(f32) for d in range(D)], axis=0).astype(bf16)
         part = product(gathered, plane[j])
         far = part if j == 0 else far + part
     half = far_out.shape[1]
     far_out[0] = far[:half]
     far_out[1] = far[half:]
-    for peer in [sibling] + peers:
-        index = index_of(peer)
-        await_in(drcv.at[index], orcv.at[index])
+    await_in(drcv.at[pl.ds(0, D - 1)], orcv)
     whole = jnp.concatenate([drcv[d] for d in range(D)], axis=0)
     density_out[0] = whole[:half]
     density_out[1] = whole[half:]
@@ -629,6 +641,7 @@
             pltpu.VMEM((n, wide, DEPTH), bf16),
             pltpu.VMEM((n, DEPTH, 2 * wide), bf16),
             pltpu.VMEM((DEPTH, own), bf16),
+            pltpu.VMEM((2, 2, wide, 2 * wide), f32),
             pltpu.VMEM((n, n, wide, wide), bf16),
             pltpu.VMEM((n, wide, own), bf16),
             pltpu.VMEM((8, n * wide), f32),
@@ -640,15 +653,15 @@
             pltpu.VMEM((D, share, own), f32),
             dma((5,)),
             dma(()),
-            dma((D,)),
+            dma((T,)),
             dma(()),
-            dma((D,)),
-            dma((n // 2, n // 2)),
-            dma((n // 2, n // 2)),
             dma(()),
-            dma((D,)),
+            dma((n // 2,)),
+            dma((n // 2,)),
             dma(()),
-            dma((D,)),
+            dma(()),
+            dma(()),
+            dma(()),
         ],
         compiler_params=pltpu.CompilerParams(
             collective_id=0, has_side_effects=True, vmem_limit_bytes=60 * 1024 * 1024),
@@ -664,7 +677,7 @@
     half = columns // 2
     f32, bf16 = jnp.float32, jnp.bfloat16
     cell_area = FOUR_PI / (own * n * 2)
-    if n <= 8 and n % 2 == 0 and columns == 4 * n and own == LANES:
+    if S == 2 and n <= 8 and columns == 4 * n and own == LANES:
         out = column_call((T, S), cell_area, points, density, incident, precond, receivers)
         return out[0].reshape(columns, own), out[1].reshape(columns, own)
     block = pltpu.VMEM((2, 2, half, own), f32)

time: 30.2 us -> 27.4 us (0.907)
  Pallas kernels: 28 us -> 25.2 us
    pallas_call x1, Pallas kernels: 28 us -> 25.2 us  [column_call(): pl.pallas_call(functools.partial(column_kernel, sizes, cell_area), out_sh...]
where the time goes in v2:
time: 27.4 us; the launch traced here: 27.2 us
  Pallas kernels  25.2 us (92%)
  local copies, waits for them, and re-layouts  1.35 us (5%)
  between operations  0.64 us (2%)
    pallas_call x1, Pallas kernels, column_call(): pl.pallas_call(functools.partial(column_kernel, sizes, cell_area), out_sh...  25.2 us
    slice x1, local copies, waits for them, and re-layouts, shards(): return (out[0].reshape(columns, own), out[1].reshape(columns, own))  1.35 us

profile of v2, /device:TPU:0, one launch (start us, length us, event | category | flops | bytes accessed | tf_op | source)
XLA Modules:
  0.0 27.2 jit_solution(15747683248910732105)
XLA Ops:
  0.6 25.2 %shard_map.68 = f32[2,2,16,128]{3,2,1,0:T(8,128)} custom-call(f32[3,128]{1,0:T(4,128)} %points.1, f32[32,128]{1,0:T(8,128)} %density.1, f32[32,128]{1,0:T(8,128)} %incident.1, f32[1,128]{1,0:T(1,128)} %bitcast.7, s32[16,1,128]{2,1,0:T(1,128)} %bitcast.6), custom_call_target="tpu_custom_call" | custom-call | tf_op jit(solution)/shard_map/pallas_call | solution.py:626
  25.8 1.3 %fusion = (f32[1,2,16,128]{3,2,1,0:T(8,128)}, f32[1,2,16,128]{3,2,1,0:T(8,128)}) fusion(f32[2,2,16,128]{3,2,1,0:T(8,128)} %shard_map.68), kind=kLoop, calls=%fused_computation | loop fusion | bytes 65536 | tf_op jit(solution)/shard_map/slice | solution.py:682

commit v3 on v2

--- a/solution.py
+++ b/solution.py
@@ -327,6 +327,7 @@
 SOFT = (TURNS * SMOOTHING) ** 2
 DEPTH = 32
 ROWS = 64
+DUE = (8, 8, 10)
 
 
 def folded(turns):
@@ -419,7 +420,7 @@
     def await_in(target, semaphore):
         pltpu.make_async_copy(target, target, semaphore).wait()
 
-    for peer in [sibling] + peers:
+    for peer in [sibling] + peers[::-1]:
         send(pmsg, pbuf.at[me], psend, prcv.at[tz], peer)
     for peer in [sibling] + peers:
         send(dmsg.at[index_of(peer)], dbuf.at[me], dsnd, drv, peer)
@@ -518,8 +519,8 @@
         following = units[i + 1] if i + 1 < len(units) else None
         if following and following[0] != k:
             plane_in(following[0])
-        if unit[0][0] == unit[0][1]:
-            for old in [k - 1] if k else []:
+        for old in range(last):
+            if i == DUE[old]:
                 await_in(swapped(old), trcv.at[old])
                 flips += [(2 * old + 1, b) for b in range(2 * old)]
         for a, b in flips:
@@ -533,6 +534,10 @@
                 swap(k, b).start()
         if i == len(units) - 2:
             columns_in()
+    for old in range(last):
+        if DUE[old] >= len(units):
+            await_in(swapped(old), trcv.at[old])
+            flips += [(2 * old + 1, b) for b in range(2 * old)]
     for a, b in flips:
         flip(a, b)
 
@@ -565,13 +570,20 @@
             update(gather_field(weighted, range(n), b), b)
         return carry
 
-    lax.fori_loop(1, ITERS, iterate, 0)
+    lax.fori_loop(1, ITERS - 1, iterate, 0)
+
+    def final_copy(k, peer):
+        block = pl.ds(S * dests[2 * k][0], S)
+        return pltpu.make_async_remote_copy(
+            wfin.at[block], wall.at[me, block], wsend, wrcv, device_id=place(peer), device_id_type=MESH)
 
     weighted = (state[...] * cell_area).astype(bf16)
-    for p in range(n):
-        wfin[spots[p]] = weighted[0:share, p * wide:(p + 1) * wide]
-    for peer in peers[::-1] + [sibling]:
-        send(wfin, wall.at[me], wsend, wrcv, peer)
+    for k in range(n // 2):
+        for p in (2 * k, 2 * k + 1):
+            update(gather_field(weighted, range(n), p), p)
+            wfin[spots[p]] = (state[0:share, p * wide:(p + 1) * wide] * cell_area).astype(bf16)
+        for peer in peers[::-1] + [sibling]:
+            final_copy(k, peer).start()
     for p in range(n):
         for s in range(2):
             dsend[2 * spots[p] + s] = state[0:share, (2 * p + s) * LANES:(2 * p + s + 1) * LANES]

time: 27.4 us -> 25.9 us (0.945)
  Pallas kernels: 25.2 us -> 23.7 us
    pallas_call x1, Pallas kernels: 25.2 us -> 23.7 us  [column_call(): pl.pallas_call(functools.partial(column_kernel, sizes, cell_area), out_sh...]
where the time goes in v3:
time: 25.9 us; the launch traced here: 25.7 us
  Pallas kernels  23.7 us (92%)
  local copies, waits for them, and re-layouts  1.35 us (5%)
  between operations  0.64 us (2%)
    pallas_call x1, Pallas kernels, column_call(): pl.pallas_call(functools.partial(column_kernel, sizes, cell_area), out_sh...  23.7 us
    slice x1, local copies, waits for them, and re-layouts, shards(): return (out[0].reshape(columns, own), out[1].reshape(columns, own))  1.35 us

profile of v3, /device:TPU:0, one launch (start us, length us, event | category | flops | bytes accessed | tf_op | source)
XLA Modules:
  0.0 25.7 jit_solution(15214991722888855936)
XLA Ops:
  0.6 23.7 %shard_map.68 = f32[2,2,16,128]{3,2,1,0:T(8,128)} custom-call(f32[3,128]{1,0:T(4,128)} %points.1, f32[32,128]{1,0:T(8,128)} %density.1, f32[32,128]{1,0:T(8,128)} %incident.1, f32[1,128]{1,0:T(1,128)} %bitcast.7, s32[16,1,128]{2,1,0:T(1,128)} %bitcast.6), custom_call_target="tpu_custom_call" | custom-call | tf_op jit(solution)/shard_map/pallas_call | solution.py:638
  24.3 1.3 %fusion = (f32[1,2,16,128]{3,2,1,0:T(8,128)}, f32[1,2,16,128]{3,2,1,0:T(8,128)}) fusion(f32[2,2,16,128]{3,2,1,0:T(8,128)} %shard_map.68), kind=kLoop, calls=%fused_computation | loop fusion | bytes 65536 | tf_op jit(solution)/shard_map/slice | solution.py:694
